TPU v7x, 32 devices: a whole 2x2x4 slice. The times are simulated.
32 devices in a mesh: ka: 16 (over z, x, core), ga: 2 (over y).
Axes of the slice: x: 2, y: 2, z: 4, core: 2. Of those that a mesh axis runs over, the one named last changes fastest.
Arguments:
- pair_density: bfloat16 [256, 64, 4096], P('ka', None, 'ga'), may hold values from -0.1875 to 0.1875
- trial_vectors: bfloat16 [256, 64, 128], P('ka'), may hold values from -6 to 6
- energy: float32 [256, 64], P('ka'), may hold values from 0.5 to 2.5
- coulomb: float32 [4096], P('ga'), may hold values from 0.03 to 0.3
- screen: bfloat16 [32, 4096, 256], P(None, 'ga'), may hold values from -0.375 to 0.375
- neighbors: int32 [256, 16], P('ka'), may hold values from 0 to 255, as said below
- live_count: int32 [256], P('ka'), may hold values from 1 to 16, as said below
- q_index: int32 [256, 16], P('ka'), may hold values from 0 to 31
Outputs:
- applied: bfloat16 [256, 64, 128], P('ka', 'ga')
Inputs may be any that keep to these rules, and one draw needn't show every extreme that they name: `neighbors`: the 16 partners of k-point k are distinct k-points whose block k' // 16 is the block of k or one of its two neighbours on the closed cycle of 16 blocks. Only the first live_count[k] slots of row k of neighbors and q_index are used; some k-point uses all 16.
All inputs are finite; a program needn't handle non-finite values.
Results may differ from a plain program's by a relative error of at most 0.013.
Values may be sent and summed in bfloat16 or wider, within the bound.
No kernel may reach another device: no remote copies, remote signals or barrier semaphores. Data moves between devices by JAX's collectives and lax.ppermute only.
A program may use at most 192 MiB of HBM per device.

v0:
```python
import jax
import jax.numpy as jnp
from jax import lax
from jax.sharding import PartitionSpec as P


def passed_along(value, axis, steps):
    count = lax.axis_size(axis)
    pairs = [(source, (source + steps) % count) for source in range(count)]
    return lax.ppermute(value, axis, pairs)


def form_products(density, vectors):
    return jnp.einsum("kpg,kpt->kgt", density, vectors, preferred_element_type=jnp.float32).astype(
        jnp.bfloat16
    )


def on_device(pair_density, trial_vectors, energy, coulomb, screen, neighbors, live_count, q_index):
    local_k, pair_count, local_g = pair_density.shape
    trial_count = trial_vectors.shape[2]
    block_size = screen.shape[2]
    groups = local_g // block_size
    cycle_size = lax.axis_size("ka")
    position = lax.axis_index("ka")
    own_products = form_products(pair_density, trial_vectors)
    below_block = passed_along(own_products, "ka", 1)
    above_block = passed_along(own_products, "ka", -1)
    window = jnp.concatenate([below_block, own_products, above_block], axis=0)
    partial_value = jnp.sum(own_products, axis=0, dtype=jnp.float32)
    density_total = lax.psum(partial_value, "ka")
    screened = coulomb[:, None] * density_total
    offset = (neighbors // local_k - position + 1) % cycle_size
    local_index = offset * local_k + neighbors % local_k

    def add_slot(slot_index, summed):
        picked = jnp.take(window, local_index[:, slot_index], axis=0)
        blocks = jnp.take(screen, q_index[:, slot_index], axis=0)
        coupled = jnp.einsum(
            "kbgc,kbct->kbgt",
            blocks.reshape(local_k, groups, block_size, block_size),
            picked.reshape(local_k, groups, block_size, trial_count),
            preferred_element_type=jnp.float32,
        ).reshape(local_k, local_g, trial_count)
        is_live = (slot_index < live_count)[:, None, None]
        return summed + jnp.where(is_live, coupled, 0.0)

    last_slot = neighbors.shape[1]
    direct = lax.fori_loop(
        0, last_slot, add_slot, jnp.zeros((local_k, local_g, trial_count), jnp.float32)
    )
    kernel = (2.0 * screened[None] - direct).astype(jnp.bfloat16)
    pair_terms = jnp.einsum(
        "kpg,kgt->kpt", pair_density, kernel, preferred_element_type=jnp.float32
    )
    mine = lax.psum_scatter(pair_terms, "ga", scatter_dimension=1, tiled=True)
    row_count = mine.shape[1]
    first_row = lax.axis_index("ga") * row_count
    energy_rows = lax.dynamic_slice_in_dim(energy, first_row, row_count, 1)
    vector_rows = lax.dynamic_slice_in_dim(trial_vectors, first_row, row_count, 1)
    return (energy_rows[:, :, None] * vector_rows.astype(jnp.float32) + mine).astype(jnp.bfloat16)


def solution(mesh):
    in_specs = (
        P("ka", None, "ga"),
        P("ka", None, None),
        P("ka", None),
        P("ga"),
        P(None, "ga", None),
        P("ka", None),
        P("ka"),
        P("ka", None),
    )
    out_specs = P("ka", "ga", None)
    return jax.shard_map(
        on_device, mesh=mesh, in_specs=in_specs, out_specs=out_specs, check_vma=False
    )
```

profile of v0, /device:TPU:0, one launch (start us, length us, event | category | flops | bytes accessed | tf_op | source)
XLA Modules:
  0.0 1172.0 jit_solution(3300030302084759185)
XLA Ops:
  23.2 165.4 %all-reduce.2.cloned.1.call-done = f32[2048,128]{1,0:T(8,128)} async-done(((f32[2048,128]{1,0:T(8,128)}), f32[2048,128]{1,0:T(8,128)}) %all-reduce.2.cloned.1.call-update) | async-done | bytes 1048592 | tf_op jit(solution)/shard_map/psum | solution.py:31
  191.1 17.6 %pad_maximum_fusion = bf16[48,2048,128]{2,1,0:T(8,128)(2,1)} fusion(bf16[16,2048,128]{2,1,0:T(8,128)(2,1)} %collective-permute-done.1, bf16[16,2048,128]{2,1,0:T(8,128)(2,1)} %get-tuple-element.182, bf16[16,2048,128]{2,1,0:T(8,128)(2,1)} %collective-permute-done), kind=kLoop, calls=%fused_computation.19 | loop fusion | flops 25165824 | bytes 50331648 | tf_op jit(solution)/shard_map/concatenate | solution.py:29
  208.7 909.0 %while.14 = (s32[]{:T(128)}, f32[16,2048,128]{2,1,0:T(8,128)}, s32[16]{0:T(128)S(1)}, s32[16,16]{0,1:T(8,128)S(1)}, bf16[32,2048,256]{2,1,0:T(8,128)(2,1)}, /*in...) while((s32[]{:T(128)}, f32[16,2048,128]{2,1,0:T(8,128)}, ...), condition=%wide.region_3.4_spmd.clone, body=%wide.region_2.3_spmd.clone.sunk | while | flops 2172651776 | bytes 142615312 | solution.py:49
  299.3 17.8 %fusion.28 = f32[16,2048,128]{2,1,0:T(8,128)} fusion(f32[16,8,256,128]{3,2,1,0:T(8,128)} %fusion.27, f32[16,2048,128]{2,1,0:T(8,128)} %get-tuple-element.244, pred[16]{0:T(512)(128)(4,1)S(1)} %broadcast_compare_fusion.2, pred[]{:T(512)S(6)} %compare.7), kind=kLoop, calls=%fused_computation.3.clone.1 | loop fusion | flops 12582912 | bytes 50331664 | tf_op jit(solution)/shard_map/while/body/eval_jaxpr/add | solution.py:46
  356.0 17.8 %fusion.28 = f32[16,2048,128]{2,1,0:T(8,128)} fusion(f32[16,8,256,128]{3,2,1,0:T(8,128)} %fusion.27, f32[16,2048,128]{2,1,0:T(8,128)} %get-tuple-element.244, pred[16]{0:T(512)(128)(4,1)S(1)} %broadcast_compare_fusion.2, pred[]{:T(512)S(6)} %compare.7), kind=kLoop, calls=%fused_computation.3.clone.1 | loop fusion | flops 12582912 | bytes 50331664 | tf_op jit(solution)/shard_map/while/body/eval_jaxpr/add | solution.py:46
  413.0 17.8 %fusion.28 = f32[16,2048,128]{2,1,0:T(8,128)} fusion(f32[16,8,256,128]{3,2,1,0:T(8,128)} %fusion.27, f32[16,2048,128]{2,1,0:T(8,128)} %get-tuple-element.244, pred[16]{0:T(512)(128)(4,1)S(1)} %broadcast_compare_fusion.2, pred[]{:T(512)S(6)} %compare.7), kind=kLoop, calls=%fused_computation.3.clone.1 | loop fusion | flops 12582912 | bytes 50331664 | tf_op jit(solution)/shard_map/while/body/eval_jaxpr/add | solution.py:46
  455.6 14.0 %fusion.27 = f32[16,8,256,128]{3,2,1,0:T(8,128)} fusion(bf16[16,8,256,256]{3,2,1,0:T(8,128)(2,1)} %bitcast.29, pred[16]{0:T(512)(128)(4,1)S(1)} %get-tuple-element.231, bf16[16,8,256,128]{3,2,1,0:T(8,128)(2,1)} %bitcast.30, pred[16]{0:T(512)(128)(4,1)S(1)} %get-tuple-element.233), kind=kOutput, calls=%fused_computation.4.clone.1 | convolution fusion | flops 2160066560 | bytes 41943072 | tf_op jit(solution)/shard_map/while/body/eval_jaxpr/kbgc,kbct->kbgt/dot_general | solution.py:39
  469.6 17.8 %fusion.28 = f32[16,2048,128]{2,1,0:T(8,128)} fusion(f32[16,8,256,128]{3,2,1,0:T(8,128)} %fusion.27, f32[16,2048,128]{2,1,0:T(8,128)} %get-tuple-element.244, pred[16]{0:T(512)(128)(4,1)S(1)} %broadcast_compare_fusion.2, pred[]{:T(512)S(6)} %compare.7), kind=kLoop, calls=%fused_computation.3.clone.1 | loop fusion | flops 12582912 | bytes 50331664 | tf_op jit(solution)/shard_map/while/body/eval_jaxpr/add | solution.py:46
  512.3 14.0 %fusion.27 = f32[16,8,256,128]{3,2,1,0:T(8,128)} fusion(bf16[16,8,256,256]{3,2,1,0:T(8,128)(2,1)} %bitcast.29, pred[16]{0:T(512)(128)(4,1)S(1)} %get-tuple-element.231, bf16[16,8,256,128]{3,2,1,0:T(8,128)(2,1)} %bitcast.30, pred[16]{0:T(512)(128)(4,1)S(1)} %get-tuple-element.233), kind=kOutput, calls=%fused_computation.4.clone.1 | convolution fusion | flops 2160066560 | bytes 41943072 | tf_op jit(solution)/shard_map/while/body/eval_jaxpr/kbgc,kbct->kbgt/dot_general | solution.py:39
  526.3 17.8 %fusion.28 = f32[16,2048,128]{2,1,0:T(8,128)} fusion(f32[16,8,256,128]{3,2,1,0:T(8,128)} %fusion.27, f32[16,2048,128]{2,1,0:T(8,128)} %get-tuple-element.244, pred[16]{0:T(512)(128)(4,1)S(1)} %broadcast_compare_fusion.2, pred[]{:T(512)S(6)} %compare.7), kind=kLoop, calls=%fused_computation.3.clone.1 | loop fusion | flops 12582912 | bytes 50331664 | tf_op jit(solution)/shard_map/while/body/eval_jaxpr/add | solution.py:46
  583.1 17.8 %fusion.28 = f32[16,2048,128]{2,1,0:T(8,128)} fusion(f32[16,8,256,128]{3,2,1,0:T(8,128)} %fusion.27, f32[16,2048,128]{2,1,0:T(8,128)} %get-tuple-element.244, pred[16]{0:T(512)(128)(4,1)S(1)} %broadcast_compare_fusion.2, pred[]{:T(512)S(6)} %compare.7), kind=kLoop, calls=%fused_computation.3.clone.1 | loop fusion | flops 12582912 | bytes 50331664 | tf_op jit(solution)/shard_map/while/body/eval_jaxpr/add | solution.py:46
  640.4 17.8 %fusion.28 = f32[16,2048,128]{2,1,0:T(8,128)} fusion(f32[16,8,256,128]{3,2,1,0:T(8,128)} %fusion.27, f32[16,2048,128]{2,1,0:T(8,128)} %get-tuple-element.244, pred[16]{0:T(512)(128)(4,1)S(1)} %broadcast_compare_fusion.2, pred[]{:T(512)S(6)} %compare.7), kind=kLoop, calls=%fused_computation.3.clone.1 | loop fusion | flops 12582912 | bytes 50331664 | tf_op jit(solution)/shard_map/while/body/eval_jaxpr/add | solution.py:46
  697.0 17.8 %fusion.28 = f32[16,2048,128]{2,1,0:T(8,128)} fusion(f32[16,8,256,128]{3,2,1,0:T(8,128)} %fusion.27, f32[16,2048,128]{2,1,0:T(8,128)} %get-tuple-element.244, pred[16]{0:T(512)(128)(4,1)S(1)} %broadcast_compare_fusion.2, pred[]{:T(512)S(6)} %compare.7), kind=kLoop, calls=%fused_computation.3.clone.1 | loop fusion | flops 12582912 | bytes 50331664 | tf_op jit(solution)/shard_map/while/body/eval_jaxpr/add | solution.py:46
  739.7 14.0 %fusion.27 = f32[16,8,256,128]{3,2,1,0:T(8,128)} fusion(bf16[16,8,256,256]{3,2,1,0:T(8,128)(2,1)} %bitcast.29, pred[16]{0:T(512)(128)(4,1)S(1)} %get-tuple-element.231, bf16[16,8,256,128]{3,2,1,0:T(8,128)(2,1)} %bitcast.30, pred[16]{0:T(512)(128)(4,1)S(1)} %get-tuple-element.233), kind=kOutput, calls=%fused_computation.4.clone.1 | convolution fusion | flops 2160066560 | bytes 41943072 | tf_op jit(solution)/shard_map/while/body/eval_jaxpr/kbgc,kbct->kbgt/dot_general | solution.py:39
  753.7 17.8 %fusion.28 = f32[16,2048,128]{2,1,0:T(8,128)} fusion(f32[16,8,256,128]{3,2,1,0:T(8,128)} %fusion.27, f32[16,2048,128]{2,1,0:T(8,128)} %get-tuple-element.244, pred[16]{0:T(512)(128)(4,1)S(1)} %broadcast_compare_fusion.2, pred[]{:T(512)S(6)} %compare.7), kind=kLoop, calls=%fused_computation.3.clone.1 | loop fusion | flops 12582912 | bytes 50331664 | tf_op jit(solution)/shard_map/while/body/eval_jaxpr/add | solution.py:46
  796.4 14.0 %fusion.27 = f32[16,8,256,128]{3,2,1,0:T(8,128)} fusion(bf16[16,8,256,256]{3,2,1,0:T(8,128)(2,1)} %bitcast.29, pred[16]{0:T(512)(128)(4,1)S(1)} %get-tuple-element.231, bf16[16,8,256,128]{3,2,1,0:T(8,128)(2,1)} %bitcast.30, pred[16]{0:T(512)(128)(4,1)S(1)} %get-tuple-element.233), kind=kOutput, calls=%fused_computation.4.clone.1 | convolution fusion | flops 2160066560 | bytes 41943072 | tf_op jit(solution)/shard_map/while/body/eval_jaxpr/kbgc,kbct->kbgt/dot_general | solution.py:39
  810.4 17.8 %fusion.28 = f32[16,2048,128]{2,1,0:T(8,128)} fusion(f32[16,8,256,128]{3,2,1,0:T(8,128)} %fusion.27, f32[16,2048,128]{2,1,0:T(8,128)} %get-tuple-element.244, pred[16]{0:T(512)(128)(4,1)S(1)} %broadcast_compare_fusion.2, pred[]{:T(512)S(6)} %compare.7), kind=kLoop, calls=%fused_computation.3.clone.1 | loop fusion | flops 12582912 | bytes 50331664 | tf_op jit(solution)/shard_map/while/body/eval_jaxpr/add | solution.py:46
  868.9 17.8 %fusion.28 = f32[16,2048,128]{2,1,0:T(8,128)} fusion(f32[16,8,256,128]{3,2,1,0:T(8,128)} %fusion.27, f32[16,2048,128]{2,1,0:T(8,128)} %get-tuple-element.244, pred[16]{0:T(512)(128)(4,1)S(1)} %broadcast_compare_fusion.2, pred[]{:T(512)S(6)} %compare.7), kind=kLoop, calls=%fused_computation.3.clone.1 | loop fusion | flops 12582912 | bytes 50331664 | tf_op jit(solution)/shard_map/while/body/eval_jaxpr/add | solution.py:46
  927.3 17.8 %fusion.28 = f32[16,2048,128]{2,1,0:T(8,128)} fusion(f32[16,8,256,128]{3,2,1,0:T(8,128)} %fusion.27, f32[16,2048,128]{2,1,0:T(8,128)} %get-tuple-element.244, pred[16]{0:T(512)(128)(4,1)S(1)} %broadcast_compare_fusion.2, pred[]{:T(512)S(6)} %compare.7), kind=kLoop, calls=%fused_computation.3.clone.1 | loop fusion | flops 12582912 | bytes 50331664 | tf_op jit(solution)/shard_map/while/body/eval_jaxpr/add | solution.py:46
  984.4 17.8 %fusion.28 = f32[16,2048,128]{2,1,0:T(8,128)} fusion(f32[16,8,256,128]{3,2,1,0:T(8,128)} %fusion.27, f32[16,2048,128]{2,1,0:T(8,128)} %get-tuple-element.244, pred[16]{0:T(512)(128)(4,1)S(1)} %broadcast_compare_fusion.2, pred[]{:T(512)S(6)} %compare.7), kind=kLoop, calls=%fused_computation.3.clone.1 | loop fusion | flops 12582912 | bytes 50331664 | tf_op jit(solution)/shard_map/while/body/eval_jaxpr/add | solution.py:46
  1042.2 17.8 %fusion.28 = f32[16,2048,128]{2,1,0:T(8,128)} fusion(f32[16,8,256,128]{3,2,1,0:T(8,128)} %fusion.27, f32[16,2048,128]{2,1,0:T(8,128)} %get-tuple-element.244, pred[16]{0:T(512)(128)(4,1)S(1)} %broadcast_compare_fusion.2, pred[]{:T(512)S(6)} %compare.7), kind=kLoop, calls=%fused_computation.3.clone.1 | loop fusion | flops 12582912 | bytes 50331664 | tf_op jit(solution)/shard_map/while/body/eval_jaxpr/add | solution.py:46
  1085.8 14.0 %fusion.27 = f32[16,8,256,128]{3,2,1,0:T(8,128)} fusion(bf16[16,8,256,256]{3,2,1,0:T(8,128)(2,1)} %bitcast.29, pred[16]{0:T(512)(128)(4,1)S(1)} %get-tuple-element.231, bf16[16,8,256,128]{3,2,1,0:T(8,128)(2,1)} %bitcast.30, pred[16]{0:T(512)(128)(4,1)S(1)} %get-tuple-element.233), kind=kOutput, calls=%fused_computation.4.clone.1 | convolution fusion | flops 2160066560 | bytes 41943072 | tf_op jit(solution)/shard_map/while/body/eval_jaxpr/kbgc,kbct->kbgt/dot_general | solution.py:39
  1099.9 17.8 %fusion.28 = f32[16,2048,128]{2,1,0:T(8,128)} fusion(f32[16,8,256,128]{3,2,1,0:T(8,128)} %fusion.27, f32[16,2048,128]{2,1,0:T(8,128)} %get-tuple-element.244, pred[16]{0:T(512)(128)(4,1)S(1)} %broadcast_compare_fusion.2, pred[]{:T(512)S(6)} %compare.7), kind=kLoop, calls=%fused_computation.3.clone.1 | loop fusion | flops 12582912 | bytes 50331664 | tf_op jit(solution)/shard_map/while/body/eval_jaxpr/add | solution.py:46
  1128.9 34.5 %reduce-scatter.2.cloned.1.call-done = f32[16,32,128]{2,1,0:T(8,128)} async-done(((f32[16,64,128]{2,1,0:T(8,128)}), f32[16,32,128]{2,1,0:T(8,128)}) %reduce-scatter.2.cloned.1.call-update) | async-done | bytes 262160 | tf_op jit(solution)/shard_map/reduce_scatter | solution.py:56
  (133 shorter events, 603.1 us)
Async XLA Ops:
  6.5 1122.3 %copy-start = (f32[16,64]{1,0:T(8,128)S(1)}, f32[16,64]{1,0:T(8,128)}, u32[]{:S(2)}) copy-start(f32[16,64]{1,0:T(8,128)} %param.12) | copy-start | bytes 12292
  6.5 182.0 %all-reduce.2.cloned.1.call-start = ((), (), s32[]{:S(2)}) async-start(), calls=%async_computation.1 | async-start | bytes 2097152 | tf_op jit(solution)/shard_map/psum | solution.py:31
  16.1 175.0 %collective-permute-start = (bf16[16,2048,128]{2,1,0:T(8,128)(2,1)}, bf16[16,2048,128]{2,1,0:T(8,128)(2,1)}, u32[]{:S(2)}, u32[]{:S(2)}) collective-permute-start(bf16[16,2048,128]{2,1,0:T(8,128)(2,1)} %get-tuple-element.182), channel_id=1, source_target_pairs={{0,2},{2,4},{4,6},{6,8},{8,10},{10,12},{12,14},{14,16},{16,18},{18... | collective-permute-start | bytes 25165832 | tf_op jit(solution)/shard_map/ppermute | solution.py:10
  16.6 174.5 %collective-permute-start.1 = (bf16[16,2048,128]{2,1,0:T(8,128)(2,1)}, bf16[16,2048,128]{2,1,0:T(8,128)(2,1)}, u32[]{:S(2)}, u32[]{:S(2)}) collective-permute-start(bf16[16,2048,128]{2,1,0:T(8,128)(2,1)} %get-tuple-element.182), channel_id=1, source_target_pairs={{0,30},{2,0},{4,2},{6,4},{8,6},{10,8},{12,10},{14,12},{16,14},{18,... | collective-permute-start | bytes 25165832 | tf_op jit(solution)/shard_map/ppermute | solution.py:10
  21.6 1141.9 %reduce-scatter.2.cloned.1.call-start = ((), (), s32[]{:S(2)}) async-start(), calls=%async_computation.2 | async-start | bytes 786432 | tf_op jit(solution)/shard_map/reduce_scatter | solution.py:56
  191.1 17.6 %copy-start.3 = (s32[16]{0:T(128)S(1)}, s32[16]{0:T(128)}, u32[]{:S(2)}) copy-start(s32[16]{0:T(128)} %param.16) | copy-start | bytes 196
  208.7 909.0 %copy-start.1 = (f32[2048,128]{1,0:T(8,128)S(1)}, f32[2048,128]{1,0:T(8,128)}, u32[]{:S(2)}) copy-start(f32[2048,128]{1,0:T(8,128)} %multiply_multiply_fusion) | copy-start | bytes 3145732
  1117.7 45.7 %copy-start.2 = (bf16[16,64,128]{2,1,0:T(8,128)(2,1)S(1)}, bf16[16,64,128]{2,1,0:T(8,128)(2,1)}, u32[]{:S(2)}) copy-start(bf16[16,64,128]{2,1,0:T(8,128)(2,1)} %param.11) | copy-start | bytes 786436
Sparse Core Ops, SparseCore 0:
  21.7 166.8 all-reduce.1
  1128.9 34.4 reduce-scatter.1
where the time goes:
time: 1170 us
  local copies, waits for them, and re-layouts  406 us (35%)
  other arithmetic  302 us (26%)
  matrix products  245 us (21%)
  waiting for transfers between devices  200 us (17%)
  between operations  13.5 us (1%)
    add x16, other arithmetic, add_slot(): return summed + jnp.where(is_live, coupled, 0.0)  279 us
    dot_general x16, matrix products, add_slot(): jnp.einsum('kbgc,kbct->kbgt', blocks.reshape(local_k, groups, block_size,...  224 us
    gather x16, local copies, waits for them, and re-layouts, add_slot(): picked = jnp.take(window, local_index[:, slot_index], axis=0)  208 us
    gather x16, local copies, waits for them, and re-layouts, add_slot(): blocks = jnp.take(screen, q_index[:, slot_index], axis=0)  197 us
    psum x1, waiting for transfers between devices, on_device(): density_total = lax.psum(partial_value, 'ka')  165 us
    reduce_scatter x1, waiting for transfers between devices, on_device(): mine = lax.psum_scatter(pair_terms, 'ga', scatter_dimension=1, tiled=True)  34.5 us
  transfers between devices with their start and end apart: 4, of which 2 were waited for; matrix products, arithmetic and copies ran while one was open for 0% of the time, Pallas kernels for 0%

commit v1 on v0

--- a/solution.py
+++ b/solution.py
@@ -2,6 +2,12 @@
 import jax.numpy as jnp
 from jax import lax
 from jax.sharding import PartitionSpec as P
+
+
+def summed_here(value, axis):
+    parts = lax.all_gather(value, axis, axis=0, tiled=False)
+    summed = parts.sum(axis=0)
+    return summed
 
 
 def passed_along(value, axis, steps):
@@ -28,7 +34,7 @@
     above_block = passed_along(own_products, "ka", -1)
     window = jnp.concatenate([below_block, own_products, above_block], axis=0)
     partial_value = jnp.sum(own_products, axis=0, dtype=jnp.float32)
-    density_total = lax.psum(partial_value, "ka")
+    density_total = summed_here(partial_value, "ka")
     screened = coulomb[:, None] * density_total
     offset = (neighbors // local_k - position + 1) % cycle_size
     local_index = offset * local_k + neighbors % local_k

time: 1170 us -> 1230 us (1.051)
  waiting for transfers between devices: 200 us -> 249 us
    psum x1 -> x0, waiting for transfers between devices: 165 us -> none  [on_device(): density_total = lax.psum(partial_value, 'ka')]
    ppermute x2, waiting for transfers between devices: 0.01 us -> 124 us  [passed_along(): return lax.ppermute(value, axis, pairs)]
    reduce_scatter x1, waiting for transfers between devices: 34.5 us -> 126 us  [on_device(): mine = lax.psum_scatter(pair_terms, 'ga', scatter_dimension=1, tiled=True)]
  transfers between devices with their start and end apart: 4 -> 4, of which waited for: 2 -> 2; matrix products, arithmetic and copies ran while one was open for 0% -> 76% of each run, Pallas kernels for 0% -> 0%
where the time goes in v1:
time: 1230 us
  local copies, waits for them, and re-layouts  407 us (33%)
  other arithmetic  307 us (25%)
  waiting for transfers between devices  249 us (20%)
  matrix products  246 us (20%)
  between operations  13.5 us (1%)
    add x16, other arithmetic, add_slot(): return summed + jnp.where(is_live, coupled, 0.0)  280 us
    dot_general x16, matrix products, add_slot(): jnp.einsum('kbgc,kbct->kbgt', blocks.reshape(local_k, groups, block_size,...  226 us
    gather x16, local copies, waits for them, and re-layouts, add_slot(): picked = jnp.take(window, local_index[:, slot_index], axis=0)  209 us
    gather x16, local copies, waits for them, and re-layouts, add_slot(): blocks = jnp.take(screen, q_index[:, slot_index], axis=0)  197 us
    reduce_scatter x1, waiting for transfers between devices, on_device(): mine = lax.psum_scatter(pair_terms, 'ga', scatter_dimension=1, tiled=True)  126 us
    ppermute x2, waiting for transfers between devices, passed_along(): return lax.ppermute(value, axis, pairs)  124 us
  transfers between devices with their start and end apart: 4, of which 2 were waited for; matrix products, arithmetic and copies ran while one was open for 76% of the time, Pallas kernels for 0%

profile of v1, /device:TPU:0, one launch (start us, length us, event | category | flops | bytes accessed | tf_op | source)
XLA Modules:
  0.0 1228.2 jit_solution(17261426957635453595)
XLA Ops:
  23.2 123.7 %collective-permute-done = bf16[16,2048,128]{2,1,0:T(8,128)(2,1)} collective-permute-done((bf16[16,2048,128]{2,1,0:T(8,128)(2,1)}, bf16[16,2048,128]{2,1,0:T(8,128)(2,1)}, u32[]{:S(2)}, u32[]{:S(2)}) %collective-permute-start) | collective-permute-done | bytes 8388640 | tf_op jit(solution)/shard_map/ppermute | solution.py:16
  146.9 18.5 %pad_maximum_fusion = bf16[48,2048,128]{2,1,0:T(8,128)(2,1)} fusion(bf16[16,2048,128]{2,1,0:T(8,128)(2,1)} %collective-permute-done.1, bf16[16,2048,128]{2,1,0:T(8,128)(2,1)} %get-tuple-element.189, bf16[16,2048,128]{2,1,0:T(8,128)(2,1)} %collective-permute-done), kind=kLoop, calls=%fused_computation.19 | loop fusion | flops 25165824 | bytes 50331648 | tf_op jit(solution)/shard_map/concatenate | solution.py:35
  165.4 911.6 %while.14 = (s32[]{:T(128)}, f32[16,2048,128]{2,1,0:T(8,128)}, s32[16]{0:T(128)S(1)}, s32[16,16]{0,1:T(8,128)S(1)}, bf16[32,2048,256]{2,1,0:T(8,128)(2,1)}, /*in...) while((s32[]{:T(128)}, f32[16,2048,128]{2,1,0:T(8,128)}, ...), condition=%wide.region_3.4_spmd.clone, body=%wide.region_2.3_spmd.clone.sunk | while | flops 2172651776 | bytes 142615312 | solution.py:55
  242.7 14.5 %fusion.27 = f32[16,8,256,128]{3,2,1,0:T(8,128)} fusion(bf16[16,8,256,256]{3,2,1,0:T(8,128)(2,1)} %bitcast.30, pred[16]{0:T(512)(128)(4,1)S(1)} %get-tuple-element.238, bf16[16,8,256,128]{3,2,1,0:T(8,128)(2,1)} %bitcast.31, pred[16]{0:T(512)(128)(4,1)S(1)} %get-tuple-element.240), kind=kOutput, calls=%fused_computation.4.clone.1 | convolution fusion | flops 2160066560 | bytes 41943072 | tf_op jit(solution)/shard_map/while/body/eval_jaxpr/kbgc,kbct->kbgt/dot_general | solution.py:45
  257.1 17.8 %fusion.28 = f32[16,2048,128]{2,1,0:T(8,128)} fusion(f32[16,8,256,128]{3,2,1,0:T(8,128)} %fusion.27, f32[16,2048,128]{2,1,0:T(8,128)} %get-tuple-element.251, pred[16]{0:T(512)(128)(4,1)S(1)} %broadcast_compare_fusion.2, pred[]{:T(512)S(6)} %compare.7), kind=kLoop, calls=%fused_computation.3.clone.1 | loop fusion | flops 12582912 | bytes 50331664 | tf_op jit(solution)/shard_map/while/body/eval_jaxpr/add | solution.py:52
  313.9 17.8 %fusion.28 = f32[16,2048,128]{2,1,0:T(8,128)} fusion(f32[16,8,256,128]{3,2,1,0:T(8,128)} %fusion.27, f32[16,2048,128]{2,1,0:T(8,128)} %get-tuple-element.251, pred[16]{0:T(512)(128)(4,1)S(1)} %broadcast_compare_fusion.2, pred[]{:T(512)S(6)} %compare.7), kind=kLoop, calls=%fused_computation.3.clone.1 | loop fusion | flops 12582912 | bytes 50331664 | tf_op jit(solution)/shard_map/while/body/eval_jaxpr/add | solution.py:52
  356.8 14.1 %fusion.27 = f32[16,8,256,128]{3,2,1,0:T(8,128)} fusion(bf16[16,8,256,256]{3,2,1,0:T(8,128)(2,1)} %bitcast.30, pred[16]{0:T(512)(128)(4,1)S(1)} %get-tuple-element.238, bf16[16,8,256,128]{3,2,1,0:T(8,128)(2,1)} %bitcast.31, pred[16]{0:T(512)(128)(4,1)S(1)} %get-tuple-element.240), kind=kOutput, calls=%fused_computation.4.clone.1 | convolution fusion | flops 2160066560 | bytes 41943072 | tf_op jit(solution)/shard_map/while/body/eval_jaxpr/kbgc,kbct->kbgt/dot_general | solution.py:45
  371.0 17.8 %fusion.28 = f32[16,2048,128]{2,1,0:T(8,128)} fusion(f32[16,8,256,128]{3,2,1,0:T(8,128)} %fusion.27, f32[16,2048,128]{2,1,0:T(8,128)} %get-tuple-element.251, pred[16]{0:T(512)(128)(4,1)S(1)} %broadcast_compare_fusion.2, pred[]{:T(512)S(6)} %compare.7), kind=kLoop, calls=%fused_computation.3.clone.1 | loop fusion | flops 12582912 | bytes 50331664 | tf_op jit(solution)/shard_map/while/body/eval_jaxpr/add | solution.py:52
  427.8 17.8 %fusion.28 = f32[16,2048,128]{2,1,0:T(8,128)} fusion(f32[16,8,256,128]{3,2,1,0:T(8,128)} %fusion.27, f32[16,2048,128]{2,1,0:T(8,128)} %get-tuple-element.251, pred[16]{0:T(512)(128)(4,1)S(1)} %broadcast_compare_fusion.2, pred[]{:T(512)S(6)} %compare.7), kind=kLoop, calls=%fused_computation.3.clone.1 | loop fusion | flops 12582912 | bytes 50331664 | tf_op jit(solution)/shard_map/while/body/eval_jaxpr/add | solution.py:52
  470.5 14.1 %fusion.27 = f32[16,8,256,128]{3,2,1,0:T(8,128)} fusion(bf16[16,8,256,256]{3,2,1,0:T(8,128)(2,1)} %bitcast.30, pred[16]{0:T(512)(128)(4,1)S(1)} %get-tuple-element.238, bf16[16,8,256,128]{3,2,1,0:T(8,128)(2,1)} %bitcast.31, pred[16]{0:T(512)(128)(4,1)S(1)} %get-tuple-element.240), kind=kOutput, calls=%fused_computation.4.clone.1 | convolution fusion | flops 2160066560 | bytes 41943072 | tf_op jit(solution)/shard_map/while/body/eval_jaxpr/kbgc,kbct->kbgt/dot_general | solution.py:45
  484.6 17.8 %fusion.28 = f32[16,2048,128]{2,1,0:T(8,128)} fusion(f32[16,8,256,128]{3,2,1,0:T(8,128)} %fusion.27, f32[16,2048,128]{2,1,0:T(8,128)} %get-tuple-element.251, pred[16]{0:T(512)(128)(4,1)S(1)} %broadcast_compare_fusion.2, pred[]{:T(512)S(6)} %compare.7), kind=kLoop, calls=%fused_computation.3.clone.1 | loop fusion | flops 12582912 | bytes 50331664 | tf_op jit(solution)/shard_map/while/body/eval_jaxpr/add | solution.py:52
  527.4 14.1 %fusion.27 = f32[16,8,256,128]{3,2,1,0:T(8,128)} fusion(bf16[16,8,256,256]{3,2,1,0:T(8,128)(2,1)} %bitcast.30, pred[16]{0:T(512)(128)(4,1)S(1)} %get-tuple-element.238, bf16[16,8,256,128]{3,2,1,0:T(8,128)(2,1)} %bitcast.31, pred[16]{0:T(512)(128)(4,1)S(1)} %get-tuple-element.240), kind=kOutput, calls=%fused_computation.4.clone.1 | convolution fusion | flops 2160066560 | bytes 41943072 | tf_op jit(solution)/shard_map/while/body/eval_jaxpr/kbgc,kbct->kbgt/dot_general | solution.py:45
  541.5 17.8 %fusion.28 = f32[16,2048,128]{2,1,0:T(8,128)} fusion(f32[16,8,256,128]{3,2,1,0:T(8,128)} %fusion.27, f32[16,2048,128]{2,1,0:T(8,128)} %get-tuple-element.251, pred[16]{0:T(512)(128)(4,1)S(1)} %broadcast_compare_fusion.2, pred[]{:T(512)S(6)} %compare.7), kind=kLoop, calls=%fused_computation.3.clone.1 | loop fusion | flops 12582912 | bytes 50331664 | tf_op jit(solution)/shard_map/while/body/eval_jaxpr/add | solution.py:52
  599.0 17.8 %fusion.28 = f32[16,2048,128]{2,1,0:T(8,128)} fusion(f32[16,8,256,128]{3,2,1,0:T(8,128)} %fusion.27, f32[16,2048,128]{2,1,0:T(8,128)} %get-tuple-element.251, pred[16]{0:T(512)(128)(4,1)S(1)} %broadcast_compare_fusion.2, pred[]{:T(512)S(6)} %compare.7), kind=kLoop, calls=%fused_computation.3.clone.1 | loop fusion | flops 12582912 | bytes 50331664 | tf_op jit(solution)/shard_map/while/body/eval_jaxpr/add | solution.py:52
  655.8 17.8 %fusion.28 = f32[16,2048,128]{2,1,0:T(8,128)} fusion(f32[16,8,256,128]{3,2,1,0:T(8,128)} %fusion.27, f32[16,2048,128]{2,1,0:T(8,128)} %get-tuple-element.251, pred[16]{0:T(512)(128)(4,1)S(1)} %broadcast_compare_fusion.2, pred[]{:T(512)S(6)} %compare.7), kind=kLoop, calls=%fused_computation.3.clone.1 | loop fusion | flops 12582912 | bytes 50331664 | tf_op jit(solution)/shard_map/while/body/eval_jaxpr/add | solution.py:52
  712.6 17.8 %fusion.28 = f32[16,2048,128]{2,1,0:T(8,128)} fusion(f32[16,8,256,128]{3,2,1,0:T(8,128)} %fusion.27, f32[16,2048,128]{2,1,0:T(8,128)} %get-tuple-element.251, pred[16]{0:T(512)(128)(4,1)S(1)} %broadcast_compare_fusion.2, pred[]{:T(512)S(6)} %compare.7), kind=kLoop, calls=%fused_computation.3.clone.1 | loop fusion | flops 12582912 | bytes 50331664 | tf_op jit(solution)/shard_map/while/body/eval_jaxpr/add | solution.py:52
  755.3 14.1 %fusion.27 = f32[16,8,256,128]{3,2,1,0:T(8,128)} fusion(bf16[16,8,256,256]{3,2,1,0:T(8,128)(2,1)} %bitcast.30, pred[16]{0:T(512)(128)(4,1)S(1)} %get-tuple-element.238, bf16[16,8,256,128]{3,2,1,0:T(8,128)(2,1)} %bitcast.31, pred[16]{0:T(512)(128)(4,1)S(1)} %get-tuple-element.240), kind=kOutput, calls=%fused_computation.4.clone.1 | convolution fusion | flops 2160066560 | bytes 41943072 | tf_op jit(solution)/shard_map/while/body/eval_jaxpr/kbgc,kbct->kbgt/dot_general | solution.py:45
  769.4 17.8 %fusion.28 = f32[16,2048,128]{2,1,0:T(8,128)} fusion(f32[16,8,256,128]{3,2,1,0:T(8,128)} %fusion.27, f32[16,2048,128]{2,1,0:T(8,128)} %get-tuple-element.251, pred[16]{0:T(512)(128)(4,1)S(1)} %broadcast_compare_fusion.2, pred[]{:T(512)S(6)} %compare.7), kind=kLoop, calls=%fused_computation.3.clone.1 | loop fusion | flops 12582912 | bytes 50331664 | tf_op jit(solution)/shard_map/while/body/eval_jaxpr/add | solution.py:52
  828.0 17.8 %fusion.28 = f32[16,2048,128]{2,1,0:T(8,128)} fusion(f32[16,8,256,128]{3,2,1,0:T(8,128)} %fusion.27, f32[16,2048,128]{2,1,0:T(8,128)} %get-tuple-element.251, pred[16]{0:T(512)(128)(4,1)S(1)} %broadcast_compare_fusion.2, pred[]{:T(512)S(6)} %compare.7), kind=kLoop, calls=%fused_computation.3.clone.1 | loop fusion | flops 12582912 | bytes 50331664 | tf_op jit(solution)/shard_map/while/body/eval_jaxpr/add | solution.py:52
  886.4 17.8 %fusion.28 = f32[16,2048,128]{2,1,0:T(8,128)} fusion(f32[16,8,256,128]{3,2,1,0:T(8,128)} %fusion.27, f32[16,2048,128]{2,1,0:T(8,128)} %get-tuple-element.251, pred[16]{0:T(512)(128)(4,1)S(1)} %broadcast_compare_fusion.2, pred[]{:T(512)S(6)} %compare.7), kind=kLoop, calls=%fused_computation.3.clone.1 | loop fusion | flops 12582912 | bytes 50331664 | tf_op jit(solution)/shard_map/while/body/eval_jaxpr/add | solution.py:52
  943.6 17.8 %fusion.28 = f32[16,2048,128]{2,1,0:T(8,128)} fusion(f32[16,8,256,128]{3,2,1,0:T(8,128)} %fusion.27, f32[16,2048,128]{2,1,0:T(8,128)} %get-tuple-element.251, pred[16]{0:T(512)(128)(4,1)S(1)} %broadcast_compare_fusion.2, pred[]{:T(512)S(6)} %compare.7), kind=kLoop, calls=%fused_computation.3.clone.1 | loop fusion | flops 12582912 | bytes 50331664 | tf_op jit(solution)/shard_map/while/body/eval_jaxpr/add | solution.py:52
  1001.5 17.8 %fusion.28 = f32[16,2048,128]{2,1,0:T(8,128)} fusion(f32[16,8,256,128]{3,2,1,0:T(8,128)} %fusion.27, f32[16,2048,128]{2,1,0:T(8,128)} %get-tuple-element.251, pred[16]{0:T(512)(128)(4,1)S(1)} %broadcast_compare_fusion.2, pred[]{:T(512)S(6)} %compare.7), kind=kLoop, calls=%fused_computation.3.clone.1 | loop fusion | flops 12582912 | bytes 50331664 | tf_op jit(solution)/shard_map/while/body/eval_jaxpr/add | solution.py:52
  1059.2 17.8 %fusion.28 = f32[16,2048,128]{2,1,0:T(8,128)} fusion(f32[16,8,256,128]{3,2,1,0:T(8,128)} %fusion.27, f32[16,2048,128]{2,1,0:T(8,128)} %get-tuple-element.251, pred[16]{0:T(512)(128)(4,1)S(1)} %broadcast_compare_fusion.2, pred[]{:T(512)S(6)} %compare.7), kind=kLoop, calls=%fused_computation.3.clone.1 | loop fusion | flops 12582912 | bytes 50331664 | tf_op jit(solution)/shard_map/while/body/eval_jaxpr/add | solution.py:52
  1094.1 125.5 %reduce-scatter.2.cloned.1.call-done = f32[16,32,128]{2,1,0:T(8,128)} async-done(((f32[16,64,128]{2,1,0:T(8,128)}), f32[16,32,128]{2,1,0:T(8,128)}) %reduce-scatter.2.cloned.1.call-update) | async-done | bytes 262160 | tf_op jit(solution)/shard_map/reduce_scatter | solution.py:62
  (134 shorter events, 608.1 us)
Async XLA Ops:
  6.5 1087.5 %copy-start = (f32[16,64]{1,0:T(8,128)S(1)}, f32[16,64]{1,0:T(8,128)}, u32[]{:S(2)}) copy-start(f32[16,64]{1,0:T(8,128)} %param.12) | copy-start | bytes 12292
  6.5 1070.5 %all-gather.3.cloned.1.call-start = ((), (), s32[]{:S(2)}) async-start(), calls=%async_computation.2 | async-start | bytes 17825792 | tf_op jit(solution)/shard_map/all_gather | solution.py:8
  16.1 130.8 %collective-permute-start = (bf16[16,2048,128]{2,1,0:T(8,128)(2,1)}, bf16[16,2048,128]{2,1,0:T(8,128)(2,1)}, u32[]{:S(2)}, u32[]{:S(2)}) collective-permute-start(bf16[16,2048,128]{2,1,0:T(8,128)(2,1)} %get-tuple-element.189), channel_id=1, source_target_pairs={{0,2},{2,4},{4,6},{6,8},{8,10},{10,12},{12,14},{14,16},{16,18},{18... | collective-permute-start | bytes 25165832 | tf_op jit(solution)/shard_map/ppermute | solution.py:16
  16.6 130.3 %collective-permute-start.1 = (bf16[16,2048,128]{2,1,0:T(8,128)(2,1)}, bf16[16,2048,128]{2,1,0:T(8,128)(2,1)}, u32[]{:S(2)}, u32[]{:S(2)}) collective-permute-start(bf16[16,2048,128]{2,1,0:T(8,128)(2,1)} %get-tuple-element.189), channel_id=1, source_target_pairs={{0,30},{2,0},{4,2},{6,4},{8,6},{10,8},{12,10},{14,12},{16,14},{18,... | collective-permute-start | bytes 25165832 | tf_op jit(solution)/shard_map/ppermute | solution.py:16
  21.6 1198.1 %reduce-scatter.2.cloned.1.call-start = ((), (), s32[]{:S(2)}) async-start(), calls=%async_computation.1 | async-start | bytes 786432 | tf_op jit(solution)/shard_map/reduce_scatter | solution.py:62
  23.2 142.2 %copy-start.3 = (s32[16]{0:T(128)S(1)}, s32[16]{0:T(128)}, u32[]{:S(2)}) copy-start(s32[16]{0:T(128)} %param.16) | copy-start | bytes 196
  1077.1 6.7 copy-start.2
  1083.8 135.9 %copy-start.1 = (bf16[16,64,128]{2,1,0:T(8,128)(2,1)S(1)}, bf16[16,64,128]{2,1,0:T(8,128)(2,1)}, u32[]{:S(2)}) copy-start(bf16[16,64,128]{2,1,0:T(8,128)(2,1)} %param.11) | copy-start | bytes 786436
Sparse Core Ops, SparseCore 0:
  21.7 229.0 all-gather.2
  1094.1 125.4 reduce-scatter.1
